TPU v7x, 512 devices: a whole 4x4x16 slice. The times are simulated.
512 devices in a mesh: section: 4 (over x_lo, core), fsdp: 32 (over x_hi, z), tensor: 4 (over y).
Axes of the slice: x: 4 (x_hi: 2, x_lo: 2; x = x_hi * 2 + x_lo), y: 4, z: 16, core: 2. Of those that a mesh axis runs over, the one named last changes fastest.
Arguments:
- entering: bfloat16 [4, 16384, 2048], P('section', 'fsdp', 'tensor'), may hold values from -8 to 8
- w_query: bfloat16 [4, 2048, 4096], P('section', 'fsdp', 'tensor'), may hold values from -0.125 to 0.125
- w_keyval: bfloat16 [4, 2048, 4, 256], P('section', 'fsdp', 'tensor'), may hold values from -0.125 to 0.125
- w_out: bfloat16 [4, 4096, 2048], P('section', 'tensor', 'fsdp'), may hold values from -0.09375 to 0.09375
Outputs:
- leaving: bfloat16 [4, 16384, 2048], P('section', 'fsdp', 'tensor')
All inputs are finite; a program needn't handle non-finite values.
Results may differ from a plain program's by a relative error of at most 0.0055.
Values may be sent and summed in bfloat16 or wider, within the bound.
A program may use at most 64 MiB of HBM per device.

v0:
```python
import math
import jax
import jax.numpy as jnp
from jax import lax
from jax.sharding import PartitionSpec as P

HEAD_DIM = 128
EPSILON = 1e-06
ROPE_BASE = 1000000.0
BEFORE_SHARE = 0.6
AFTER_SHARE = 0.4


def shifted(block, axis, distance):
    devices = range(lax.axis_size(axis))
    route = [((i - distance) % len(devices), i) for i in devices]
    return lax.ppermute(block, axis, route)


def rope_tables(length, width):
    half_width = width // 2
    exponent = jnp.arange(half_width, dtype=jnp.float32) * (2.0 / width)
    inverse = jnp.exp(-exponent * math.log(ROPE_BASE))
    angles = jnp.arange(length, dtype=jnp.float32)[:, None] * inverse[None, :]
    return (jnp.cos(angles)[:, None, :], jnp.sin(angles)[:, None, :])


def head_norm_rope(vectors, cosine, sine):
    meansq = jnp.mean(vectors * vectors, axis=-1, keepdims=True)
    normed = vectors * lax.rsqrt(meansq + EPSILON)
    half_width = vectors.shape[-1] // 2
    first_half = normed[..., :half_width]
    second_half = normed[..., half_width:]
    return jnp.concatenate(
        [first_half * cosine - second_half * sine, second_half * cosine + first_half * sine],
        axis=-1,
    )


def pack_weights(query_shard, keyval_shard, out_shard):
    return jnp.concatenate(
        [query_shard.reshape(1, -1), keyval_shard.reshape(1, -1), out_shard.reshape(1, -1)], axis=1
    )


def body(entering, w_query, w_keyval, w_out):
    owned_pack = pack_weights(w_query, w_keyval, w_out)
    from_lower = shifted(owned_pack, "section", 1)
    from_upper = shifted(owned_pack, "section", -1)
    section_pack = (
        BEFORE_SHARE * from_lower.astype(jnp.float32) + AFTER_SHARE * from_upper.astype(jnp.float32)
    ).astype(jnp.bfloat16)
    query_count = w_query.size
    keyval_count = w_keyval.size
    query_mine = section_pack[:, :query_count].reshape(w_query.shape)
    keyval_mine = section_pack[:, query_count : query_count + keyval_count].reshape(w_keyval.shape)
    out_mine = section_pack[:, query_count + keyval_count :].reshape(w_out.shape)
    own_rows = entering[0]
    own_float = own_rows.astype(jnp.float32)
    full_rows = lax.all_gather(own_rows, "tensor", axis=1, tiled=True).astype(jnp.float32)
    meansq = jnp.mean(full_rows * full_rows, axis=-1, keepdims=True)
    normed = (full_rows * lax.rsqrt(meansq + EPSILON)).astype(jnp.bfloat16)
    length = normed.shape[0]
    query_width = query_mine.shape[2]
    keyval_width = keyval_mine.shape[2] * keyval_mine.shape[3]
    query_piece = lax.all_gather(query_mine, "fsdp", axis=1, tiled=True)
    keyval_piece = lax.all_gather(keyval_mine, "fsdp", axis=1, tiled=True)
    piece_rows = query_piece.shape[1]
    query_sum = jnp.dot(normed, query_piece[0], preferred_element_type=jnp.float32)
    keyval_sum = jnp.dot(
        normed, keyval_piece[0].reshape(piece_rows, -1), preferred_element_type=jnp.float32
    )
    query_heads = query_width // HEAD_DIM
    kv_count = keyval_width // (2 * HEAD_DIM)
    group_size = query_heads // kv_count
    cosine, sine = rope_tables(length, HEAD_DIM)
    queries = head_norm_rope(
        query_sum.reshape(length, kv_count, group_size, HEAD_DIM),
        cosine[:, :, None, :],
        sine[:, :, None, :],
    ).astype(jnp.bfloat16)
    keyval_heads = keyval_sum.reshape(length, kv_count, 2 * HEAD_DIM)
    keys = head_norm_rope(keyval_heads[..., :HEAD_DIM], cosine, sine).astype(jnp.bfloat16)
    values = keyval_heads[..., HEAD_DIM:].astype(jnp.bfloat16)
    positions = jnp.arange(length)
    causal = positions[:, None] >= positions[None, :]
    scale = 1.0 / math.sqrt(HEAD_DIM)

    def one_group(query_slice):
        scores = (
            jnp.einsum("qkd,pkd->kqp", query_slice, keys, preferred_element_type=jnp.float32)
            * scale
        )
        expo = jnp.where(causal[None], jnp.exp(scores - math.sqrt(HEAD_DIM)), 0.0)
        weights = (expo / jnp.sum(expo, axis=-1, keepdims=True)).astype(jnp.bfloat16)
        return jnp.einsum(
            "kqp,pkd->qkd", weights, values, preferred_element_type=jnp.float32
        ).astype(jnp.bfloat16)

    mixed = lax.map(one_group, jnp.moveaxis(queries, 2, 0))
    mixed = jnp.moveaxis(mixed, 0, 2).reshape(length, query_heads * HEAD_DIM)
    partial_terms = jnp.dot(
        mixed,
        lax.all_gather(out_mine, "fsdp", axis=2, tiled=True)[0],
        preferred_element_type=jnp.float32,
    ).astype(jnp.bfloat16)
    summed = lax.psum_scatter(partial_terms, "tensor", scatter_dimension=1, tiled=True).astype(
        jnp.float32
    )
    return (own_float + summed).astype(jnp.bfloat16)[None]


def solution(mesh):
    in_specs = (
        P("section", "fsdp", "tensor"),
        P("section", "fsdp", "tensor"),
        P("section", "fsdp", "tensor", None),
        P("section", "tensor", "fsdp"),
    )
    out_specs = P("section", "fsdp", "tensor")
    return jax.shard_map(body, mesh=mesh, in_specs=in_specs, out_specs=out_specs, check_vma=False)
```

profile of v0, /device:TPU:1, one launch (start us, length us, event | category | flops | bytes accessed | tf_op | source)
XLA Modules:
  0.0 575.0 jit_solution(11576316620218176375)
XLA Ops:
  6.5 1.1 copy.29
  7.9 0.8 copy.30
  8.7 1.1 copy.20
  10.4 4.5 collective-permute-start
  14.9 6.2 %collective-permute-start.1 = (bf16[1,147456]{1,0:T(2,128)(2,1)S(1)}, bf16[1,147456]{1,0:T(2,128)(2,1)S(1)}, u32[]{:S(2)}, u32[]{:S(2)}) collective-permute-start(bf16[1,147456]{1,0:T(2,128)(2,1)S(1)} %constant_dynamic-update-slice_fusion.1), channel_id=1, source_target_pairs={{128,0},{256,128},{384,256},{0,384},{129,1},{257,129},{385,257},{1... | collective-permute-start | bytes 884744 | tf_op jit(solution)/shard_map/ppermute | solution.py:17
  21.1 0.6 collective-permute-done
  21.7 9.4 %collective-permute-done.1 = bf16[1,147456]{1,0:T(2,128)(2,1)S(1)} collective-permute-done((bf16[1,147456]{1,0:T(2,128)(2,1)S(1)}, bf16[1,147456]{1,0:T(2,128)(2,1)S(1)}, u32[]{:S(2)}, u32[]{:S(2)}) %collective-permute-start.1) | collective-permute-done | bytes 294944 | tf_op jit(solution)/shard_map/ppermute | solution.py:17
  31.0 1.4 add_convert_fusion.1
  32.7 0.6 reshape.283
  33.4 1.5 slice_reduce_fusion
  34.9 0.7 reshape.281
  35.7 1.0 fusion.29
  36.8 0.8 copy.26
  37.8 21.9 %all-gather.12.cloned.1.call-done = bf16[1,512,2048]{2,1,0:T(8,128)(2,1)} async-done(((bf16[1,512,512]{2,1,0:T(8,128)(2,1)}), bf16[1,512,2048]{2,1,0:T(8,128)(2,1)}) %all-gather.12.cloned.1.call-update) | async-done | bytes 2097168 | tf_op jit(solution)/shard_map/all_gather | solution.py:60
  59.7 2.2 fusion.11
  62.0 135.2 %all-gather.8.cloned.1.call-done = bf16[1,2048,1,256]{3,1,2,0:T(8,128)(2,1)} async-done(((bf16[1,64,1,256]{3,1,2,0:T(8,128)(2,1)}), bf16[1,2048,1,256]{3,1,2,0:T(8,128)(2,1)}) %all-gather.8.cloned.1.call-update) | async-done | bytes 1048592 | tf_op jit(solution)/shard_map/all_gather | solution.py:67
  197.2 2.1 convolution_bitcast_fusion
  199.4 0.6 subtract_convert_fusion.1
  200.2 157.7 %all-gather.6.cloned.1.call-done = bf16[1,2048,1024]{2,1,0:T(8,128)(2,1)} async-done(((bf16[1,64,1024]{2,1,0:T(8,128)(2,1)}), bf16[1,2048,1024]{2,1,0:T(8,128)(2,1)}) %all-gather.6.cloned.1.call-update) | async-done | bytes 4194320 | tf_op jit(solution)/shard_map/all_gather | solution.py:66
  358.0 4.6 fusion.20
  362.5 0.5 copy.31
  363.0 0.6 multiply_reduce_fusion
  363.7 0.6 copy_multiply_fusion
  364.4 0.8 subtract_convert_fusion
  365.1 0.6 maximum_bitcast_fusion
  365.7 0.6 copy-done.2
  366.4 6.8 %while.13 = (s32[]{:T(128)}, bf16[8,512,1,128]{1,3,0,2:T(8,128)(2,1)S(1)}, bf16[8,512,1,128]{3,1,2,0:T(8,128)(2,1)S(1)}, bf16[512,1,128]{2,0,1:T(8,128)(2,1)S(1)}, bf16[512,1,128]{2,0,1:T(8,128)(2,1)S(1)}, /*index=5*/s32[]{:T(128)}) while((s32[]{:T(128)}, bf16[8,512,1,128]{1,3,0,2:T(8,128)(2,1)S(1)}, ...), condition=%wide.region_5.6_spmd.clone, body=%wide.region_3.5_spmd.clone.sunk | while | flops 136117760 | bytes 3149901 | solution.py:100
  367.5 0.4 fusion.39
  373.2 146.0 %all-gather.10.cloned.1.call-done = bf16[1,1024,2048]{1,2,0:T(8,128)(2,1)} async-done(((bf16[1,1024,64]{1,2,0:T(8,128)(2,1)}), bf16[1,1024,2048]{1,2,0:T(8,128)(2,1)}) %all-gather.10.cloned.1.call-update) | async-done | bytes 4194320 | tf_op jit(solution)/shard_map/all_gather | solution.py:104
  519.1 5.9 %fusion.17 = bf16[512,2048]{1,0:T(8,128)(2,1)} fusion(bf16[512,1024]{0,1:T(8,128)(2,1)S(1)} %bitcast.78, bf16[1,1024,2048]{1,2,0:T(8,128)(2,1)} %all-gather.10.cloned.1.call-done), kind=kOutput, calls=%fused_computation.23 | convolution fusion | flops 2148532224 | bytes 7340032 | tf_op jit(solution)/shard_map/dot_general | solution.py:102
  525.0 41.4 %reduce-scatter.2.cloned.1.call-done = bf16[512,512]{1,0:T(8,128)(2,1)} async-done(((bf16[512,2048]{1,0:T(8,128)(2,1)}), bf16[512,512]{1,0:T(8,128)(2,1)}) %reduce-scatter.2.cloned.1.call-update) | async-done | bytes 524304 | tf_op jit(solution)/shard_map/reduce_scatter | solution.py:107
  566.5 2.0 fusion.27
  (64 shorter events, 8.2 us)
Async XLA Ops:
  6.5 53.2 %all-gather.12.cloned.1.call-start = ((), (), s32[]{:S(2)}) async-start(), calls=%async_computation.5 | async-start | bytes 2621440 | tf_op jit(solution)/shard_map/all_gather | solution.py:60
  10.4 11.3 %collective-permute-start = (bf16[1,147456]{1,0:T(2,128)(2,1)S(1)}, bf16[1,147456]{1,0:T(2,128)(2,1)S(1)}, u32[]{:S(2)}, u32[]{:S(2)}) collective-permute-start(bf16[1,147456]{1,0:T(2,128)(2,1)S(1)} %constant_dynamic-update-slice_fusion.1), channel_id=1, source_target_pairs={{384,0},{0,128},{128,256},{256,384},{385,1},{1,129},{129,257},{257... | collective-permute-start | bytes 884744 | tf_op jit(solution)/shard_map/ppermute | solution.py:17
  14.9 16.2 %collective-permute-start.1 = (bf16[1,147456]{1,0:T(2,128)(2,1)S(1)}, bf16[1,147456]{1,0:T(2,128)(2,1)S(1)}, u32[]{:S(2)}, u32[]{:S(2)}) collective-permute-start(bf16[1,147456]{1,0:T(2,128)(2,1)S(1)} %constant_dynamic-update-slice_fusion.1), channel_id=1, source_target_pairs={{128,0},{256,128},{384,256},{0,384},{129,1},{257,129},{385,257},{1... | collective-permute-start | bytes 884744 | tf_op jit(solution)/shard_map/ppermute | solution.py:17
  21.1 176.1 %all-gather.8.cloned.1.call-start = ((), (), s32[]{:S(2)}) async-start(), calls=%async_computation.2 | async-start | bytes 1081344 | tf_op jit(solution)/shard_map/all_gather | solution.py:67
  33.3 324.6 %all-gather.6.cloned.1.call-start = ((), (), s32[]{:S(2)}) async-start(), calls=%async_computation.1 | async-start | bytes 4325376 | tf_op jit(solution)/shard_map/all_gather | solution.py:66
  35.6 483.5 %all-gather.10.cloned.1.call-start = ((), (), s32[]{:S(2)}) async-start(), calls=%async_computation.3 | async-start | bytes 4325376 | tf_op jit(solution)/shard_map/all_gather | solution.py:104
  37.6 528.8 %reduce-scatter.2.cloned.1.call-start = ((), (), s32[]{:S(2)}) async-start(), calls=%async_computation.4 | async-start | bytes 2621440 | tf_op jit(solution)/shard_map/reduce_scatter | solution.py:107
  59.7 137.5 %copy-start.1 = (bf16[1,512,2048]{2,1,0:T(8,128)(2,1)S(1)}, bf16[1,512,2048]{2,1,0:T(8,128)(2,1)}, u32[]{:S(2)}) copy-start(bf16[1,512,2048]{2,1,0:T(8,128)(2,1)} %all-gather.12.cloned.1.call-done) | copy-start | bytes 6291460
  365.1 1.2 copy-start.2
  525.0 41.4 %copy-start = (bf16[1,512,512]{2,1,0:T(8,128)(2,1)S(1)}, bf16[1,512,512]{2,1,0:T(8,128)(2,1)}, u32[]{:S(2)}) copy-start(bf16[1,512,512]{2,1,0:T(8,128)(2,1)} %param.6) | copy-start | bytes 1572868
Sparse Core Ops, SparseCore 0:
  21.2 38.4 all-gather.11
  62.8 134.3 all-gather.7
  200.3 157.6 all-gather.5
  360.9 158.1 all-gather.9
  525.2 41.2 reduce-scatter.1
where the time goes:
time: 575 us
  waiting for transfers between devices  512 us (89%)
  matrix products  18 us (3%)
  between operations  13.4 us (2%)
  starting transfers between devices  11 us (2%)
  local copies, waits for them, and re-layouts  10.2 us (2%)
  other arithmetic  9.86 us (2%)
    all_gather x1, waiting for transfers between devices, body(): query_piece = lax.all_gather(query_mine, 'fsdp', axis=1, tiled=True)  158 us
    all_gather x1, waiting for transfers between devices, body(): lax.all_gather(out_mine, 'fsdp', axis=2, tiled=True)[0]  146 us
    all_gather x1, waiting for transfers between devices, body(): keyval_piece = lax.all_gather(keyval_mine, 'fsdp', axis=1, tiled=True)  135 us
    reduce_scatter x1, waiting for transfers between devices, body(): lax.psum_scatter(partial_terms, 'tensor', scatter_dimension=1, tiled=True)  41.4 us
    all_gather x1, waiting for transfers between devices, body(): lax.all_gather(own_rows, 'tensor', axis=1, tiled=True).astype(jnp.float32)  21.9 us
  transfers between devices with their start and end apart: 7, of which 7 were waited for; matrix products, arithmetic and copies ran while one was open for 4% of the time, Pallas kernels for 0%

commit v1 on v0

--- a/solution.py
+++ b/solution.py
@@ -64,7 +64,9 @@
     query_width = query_mine.shape[2]
     keyval_width = keyval_mine.shape[2] * keyval_mine.shape[3]
     query_piece = lax.all_gather(query_mine, "fsdp", axis=1, tiled=True)
-    keyval_piece = lax.all_gather(keyval_mine, "fsdp", axis=1, tiled=True)
+    keyval_piece = jnp.concatenate(
+        lax.all_to_all(jnp.stack([keyval_mine] * lax.axis_size("fsdp")), "fsdp", 0, 0), axis=1
+    )
     piece_rows = query_piece.shape[1]
     query_sum = jnp.dot(normed, query_piece[0], preferred_element_type=jnp.float32)
     keyval_sum = jnp.dot(

time: 575 us -> 442 us (0.77)
  waiting for transfers between devices: 512 us -> 363 us
  starting transfers between devices: 11 us -> 26.3 us
    all_gather x1 -> x0, waiting for transfers between devices: 135 us -> none  [body(): keyval_piece = lax.all_gather(keyval_mine, 'fsdp', axis=1, tiled=True)]
    all_to_all x0 -> x1, waiting for transfers between devices: none -> 45 us  [body(): lax.all_to_all(jnp.stack([keyval_mine] * lax.axis_size('fsdp')), 'fsdp',...]
    all_gather x1, waiting for transfers between devices: 158 us -> 115 us  [body(): query_piece = lax.all_gather(query_mine, 'fsdp', axis=1, tiled=True)]
    all_gather x1, waiting for transfers between devices: 21.9 us -> 5.44 us  [body(): lax.all_gather(own_rows, 'tensor', axis=1, tiled=True).astype(jnp.float32)]
    all_to_all x0 -> x1, starting transfers between devices: none -> 15.3 us  [body(): lax.all_to_all(jnp.stack([keyval_mine] * lax.axis_size('fsdp')), 'fsdp',...]
  transfers between devices with their start and end apart: 7 -> 7, of which waited for: 7 -> 7; matrix products, arithmetic and copies ran while one was open for 4% -> 6% of each run, Pallas kernels for 0% -> 0%
where the time goes in v1:
time: 442 us
  waiting for transfers between devices  363 us (82%)
  starting transfers between devices  26.3 us (6%)
  matrix products  16.9 us (4%)
  between operations  13.4 us (3%)
  local copies, waits for them, and re-layouts  11.7 us (3%)
  other arithmetic  10.6 us (2%)
    all_gather x1, waiting for transfers between devices, body(): lax.all_gather(out_mine, 'fsdp', axis=2, tiled=True)[0]  146 us
    all_gather x1, waiting for transfers between devices, body(): query_piece = lax.all_gather(query_mine, 'fsdp', axis=1, tiled=True)  115 us
    all_to_all x1, waiting for transfers between devices, body(): lax.all_to_all(jnp.stack([keyval_mine] * lax.axis_size('fsdp')), 'fsdp',...  45 us
    reduce_scatter x1, waiting for transfers between devices, body(): lax.psum_scatter(partial_terms, 'tensor', scatter_dimension=1, tiled=True)  41.4 us
    all_to_all x1, starting transfers between devices, body(): lax.all_to_all(jnp.stack([keyval_mine] * lax.axis_size('fsdp')), 'fsdp',...  15.3 us
    ppermute x2, starting transfers between devices, shifted(): return lax.ppermute(block, axis, route)  10.7 us
    ppermute x2, waiting for transfers between devices, shifted(): return lax.ppermute(block, axis, route)  9.92 us
  transfers between devices with their start and end apart: 7, of which 7 were waited for; matrix products, arithmetic and copies ran while one was open for 6% of the time, Pallas kernels for 0%

profile of v1, /device:TPU:1, one launch (start us, length us, event | category | flops | bytes accessed | tf_op | source)
XLA Modules:
  0.0 442.0 jit_solution(9930856259666038818)
XLA Ops:
  6.5 1.1 copy.29
  7.9 0.8 copy.30
  8.7 1.1 copy.20
  10.4 4.5 %collective-permute-start = (bf16[1,147456]{1,0:T(2,128)(2,1)S(1)}, bf16[1,147456]{1,0:T(2,128)(2,1)S(1)}, u32[]{:S(2)}, u32[]{:S(2)}) collective-permute-start(bf16[1,147456]{1,0:T(2,128)(2,1)S(1)} %constant_dynamic-update-slice_fusion.1), channel_id=1, source_target_pairs={{384,0},{0,128},{128,256},{256,384},{385,1},{1,129},{129,257},{257... | collective-permute-start | bytes 884744 | tf_op jit(solution)/shard_map/ppermute | solution.py:17
  14.9 6.2 %collective-permute-start.1 = (bf16[1,147456]{1,0:T(2,128)(2,1)S(1)}, bf16[1,147456]{1,0:T(2,128)(2,1)S(1)}, u32[]{:S(2)}, u32[]{:S(2)}) collective-permute-start(bf16[1,147456]{1,0:T(2,128)(2,1)S(1)} %constant_dynamic-update-slice_fusion.1), channel_id=1, source_target_pairs={{128,0},{256,128},{384,256},{0,384},{129,1},{257,129},{385,257},{1... | collective-permute-start | bytes 884744 | tf_op jit(solution)/shard_map/ppermute | solution.py:17
  21.1 0.6 collective-permute-done
  21.7 9.4 %collective-permute-done.1 = bf16[1,147456]{1,0:T(2,128)(2,1)S(1)} collective-permute-done((bf16[1,147456]{1,0:T(2,128)(2,1)S(1)}, bf16[1,147456]{1,0:T(2,128)(2,1)S(1)}, u32[]{:S(2)}, u32[]{:S(2)}) %collective-permute-start.1) | collective-permute-done | bytes 294944 | tf_op jit(solution)/shard_map/ppermute | solution.py:17
  31.0 1.4 add_convert_fusion.1
  32.5 1.5 slice_reduce_fusion
  34.0 0.7 reshape.282
  34.9 1.1 stack.3
  36.0 15.3 %all-to-all-start = ((bf16[32,1,64,1,256]{4,2,3,1,0:T(8,128)(2,1)}), bf16[32,1,64,1,256]{4,2,3,1,0:T(8,128)(2,1)S(1)}, u32[]{:S(2)}, u32[]{:S(2)}) async-start(bf16[32,1,64,1,256]{4,2,3,1,0:T(8,128)(2,1)} %stack.3), calls=%async_computation | async-start | bytes 2097152 | tf_op jit(solution)/shard_map/all_to_all | solution.py:68
  51.4 1.7 fusion.28
  53.2 0.8 copy.26
  54.3 5.4 %all-gather.9.cloned.1.call-done = bf16[1,512,2048]{2,1,0:T(8,128)(2,1)} async-done(((bf16[1,512,512]{2,1,0:T(8,128)(2,1)}), bf16[1,512,2048]{2,1,0:T(8,128)(2,1)}) %all-gather.9.cloned.1.call-update) | async-done | bytes 2097168 | tf_op jit(solution)/shard_map/all_gather | solution.py:60
  59.7 2.2 fusion.11
  62.0 45.0 %all-to-all-done = bf16[32,1,64,1,256]{4,2,3,1,0:T(8,128)(2,1)S(1)} async-done(((bf16[32,1,64,1,256]{4,2,3,1,0:T(8,128)(2,1)}), bf16[32,1,64,1,256]{4,2,3,1,0:T(8,128)(2,1)S(1)}, u32[]{:S(2)}, u32[]{:S(2)}) %all-to-all-start) | async-done | bytes 1048608 | tf_op jit(solution)/shard_map/all_to_all | solution.py:68
  106.9 0.9 convolution_bitcast_fusion
  108.0 0.6 subtract_convert_fusion.1
  108.7 0.8 copy.24
  109.4 115.4 %all-gather.5.cloned.1.call-done = bf16[1,2048,1024]{2,1,0:T(8,128)(2,1)} async-done(((bf16[1,64,1024]{2,1,0:T(8,128)(2,1)}), bf16[1,2048,1024]{2,1,0:T(8,128)(2,1)}) %all-gather.5.cloned.1.call-update) | async-done | bytes 4194320 | tf_op jit(solution)/shard_map/all_gather | solution.py:66
  224.8 4.6 %fusion.20 = f32[64,8,8,128]{3,1,2,0:T(8,128)S(1)} fusion(bf16[1,2048,1024]{2,1,0:T(8,128)(2,1)} %all-gather.5.cloned.1.call-done, bf16[1,512,2048]{2,1,0:T(8,128)(2,1)S(1)} %copy-done.1, f32[512]{0:T(512)S(1)} %add_rsqrt_fusion.2), kind=kOutput, calls=%fused_computation.28 | convolution fusion | flops 2150629376 | bytes 8390656 | tf_op jit(solution)/shard_map/dot_general | solution.py:71
  229.4 0.5 copy.31
  229.9 0.6 multiply_reduce_fusion
  230.7 0.6 copy_multiply_fusion
  231.6 0.8 subtract_convert_fusion
  232.4 0.6 maximum_bitcast_fusion
  233.7 6.8 %while.13 = (s32[]{:T(128)}, bf16[8,512,1,128]{1,3,0,2:T(8,128)(2,1)S(1)}, bf16[8,512,1,128]{3,1,2,0:T(8,128)(2,1)S(1)}, bf16[512,1,128]{2,0,1:T(8,128)(2,1)S(1)}, bf16[512,1,128]{2,0,1:T(8,128)(2,1)S(1)}, /*index=5*/s32[]{:T(128)}) while((s32[]{:T(128)}, bf16[8,512,1,128]{1,3,0,2:T(8,128)(2,1)S(1)}, ...), condition=%wide.region_5.6_spmd.clone, body=%wide.region_3.5_spmd.clone.sunk | while | flops 136117760 | bytes 3149901 | solution.py:102
  240.5 145.7 %all-gather.7.cloned.1.call-done = bf16[1,1024,2048]{1,2,0:T(8,128)(2,1)} async-done(((bf16[1,1024,64]{1,2,0:T(8,128)(2,1)}), bf16[1,1024,2048]{1,2,0:T(8,128)(2,1)}) %all-gather.7.cloned.1.call-update) | async-done | bytes 4194320 | tf_op jit(solution)/shard_map/all_gather | solution.py:106
  386.1 5.9 %fusion.17 = bf16[512,2048]{1,0:T(8,128)(2,1)} fusion(bf16[512,1024]{0,1:T(8,128)(2,1)S(1)} %bitcast.78, bf16[1,1024,2048]{1,2,0:T(8,128)(2,1)} %all-gather.7.cloned.1.call-done), kind=kOutput, calls=%fused_computation.23 | convolution fusion | flops 2148532224 | bytes 7340032 | tf_op jit(solution)/shard_map/dot_general | solution.py:104
  392.0 41.4 %reduce-scatter.2.cloned.1.call-done = bf16[512,512]{1,0:T(8,128)(2,1)} async-done(((bf16[512,2048]{1,0:T(8,128)(2,1)}), bf16[512,512]{1,0:T(8,128)(2,1)}) %reduce-scatter.2.cloned.1.call-update) | async-done | bytes 524304 | tf_op jit(solution)/shard_map/reduce_scatter | solution.py:109
  433.5 2.0 fusion.26
  (68 shorter events, 9.4 us)
Async XLA Ops:
  6.5 53.2 %all-gather.9.cloned.1.call-start = ((), (), s32[]{:S(2)}) async-start(), calls=%async_computation.5 | async-start | bytes 2621440 | tf_op jit(solution)/shard_map/all_gather | solution.py:60
  10.4 11.3 %collective-permute-start = (bf16[1,147456]{1,0:T(2,128)(2,1)S(1)}, bf16[1,147456]{1,0:T(2,128)(2,1)S(1)}, u32[]{:S(2)}, u32[]{:S(2)}) collective-permute-start(bf16[1,147456]{1,0:T(2,128)(2,1)S(1)} %constant_dynamic-update-slice_fusion.1), channel_id=1, source_target_pairs={{384,0},{0,128},{128,256},{256,384},{385,1},{1,129},{129,257},{257... | collective-permute-start | bytes 884744 | tf_op jit(solution)/shard_map/ppermute | solution.py:17
  14.9 16.2 %collective-permute-start.1 = (bf16[1,147456]{1,0:T(2,128)(2,1)S(1)}, bf16[1,147456]{1,0:T(2,128)(2,1)S(1)}, u32[]{:S(2)}, u32[]{:S(2)}) collective-permute-start(bf16[1,147456]{1,0:T(2,128)(2,1)S(1)} %constant_dynamic-update-slice_fusion.1), channel_id=1, source_target_pairs={{128,0},{256,128},{384,256},{0,384},{129,1},{257,129},{385,257},{1... | collective-permute-start | bytes 884744 | tf_op jit(solution)/shard_map/ppermute | solution.py:17
  21.1 203.8 %all-gather.5.cloned.1.call-start = ((), (), s32[]{:S(2)}) async-start(), calls=%async_computation.2 | async-start | bytes 4325376 | tf_op jit(solution)/shard_map/all_gather | solution.py:66
  36.0 70.9 %all-to-all-start = ((bf16[32,1,64,1,256]{4,2,3,1,0:T(8,128)(2,1)}), bf16[32,1,64,1,256]{4,2,3,1,0:T(8,128)(2,1)S(1)}, u32[]{:S(2)}, u32[]{:S(2)}) async-start(bf16[32,1,64,1,256]{4,2,3,1,0:T(8,128)(2,1)} %stack.3), calls=%async_computation | async-start | bytes 2097152 | tf_op jit(solution)/shard_map/all_to_all | solution.py:68
  51.3 334.8 %all-gather.7.cloned.1.call-start = ((), (), s32[]{:S(2)}) async-start(), calls=%async_computation.3 | async-start | bytes 4325376 | tf_op jit(solution)/shard_map/all_gather | solution.py:106
  54.0 379.4 %reduce-scatter.2.cloned.1.call-start = ((), (), s32[]{:S(2)}) async-start(), calls=%async_computation.4 | async-start | bytes 2621440 | tf_op jit(solution)/shard_map/reduce_scatter | solution.py:109
  59.7 47.2 %copy-start.1 = (bf16[1,512,2048]{2,1,0:T(8,128)(2,1)S(1)}, bf16[1,512,2048]{2,1,0:T(8,128)(2,1)}, u32[]{:S(2)}) copy-start(bf16[1,512,2048]{2,1,0:T(8,128)(2,1)} %all-gather.9.cloned.1.call-done) | copy-start | bytes 6291460
  230.7 1.0 copy-start.2
  232.4 0.9 copy-start.3
  232.4 1.3 copy-start.4
  392.0 41.4 %copy-start = (bf16[1,512,512]{2,1,0:T(8,128)(2,1)S(1)}, bf16[1,512,512]{2,1,0:T(8,128)(2,1)}, u32[]{:S(2)}) copy-start(bf16[1,512,512]{2,1,0:T(8,128)(2,1)} %param.6) | copy-start | bytes 1572868
Sparse Core Ops, SparseCore 0:
  21.2 38.4 all-gather.8
  62.8 161.9 all-gather.4
  228.0 158.1 all-gather.6
  392.2 41.2 reduce-scatter.1
